TPU v7x, 32 devices: a whole 2x2x4 slice. The times are simulated.
32 devices in a mesh: depth: 8 (over z, y), xline: 4 (over x, core).
Axes of the slice: x: 2, y: 2, z: 4, core: 2. Of those that a mesh axis runs over, the one named last changes fastest.
Arguments:
- surface_fields: float32 [2, 2, 2, 64, 128], P(None, None, None, 'xline'), may hold values from -6 to 6
- stencil_table: float32 [13, 2, 2, 128], replicated
- velocity_bins: int32 [8, 2, 64, 128], P('depth', None, 'xline'), may hold values from 0 to 127
- offset_list: int32 [16, 2], replicated, may hold values from -8 to 8, as said below
Outputs:
- image_tiles: float32 [8, 16, 64, 128], P('depth', None, 'xline')
Inputs may be any that keep to these rules, and one draw needn't show every extreme that they name: `offset_list`: column 0 lies within -8 to 8 and column 1 within -8 to 8; both ends of both ranges occur in every draw.
All inputs are finite; a program needn't handle non-finite values.
Results may differ from a plain program's by a relative error of at most 0.0003.
Values sent between devices are 32-bit elements; how exact they have to be, the bound alone decides.
No kernel may reach another device: no remote copies, remote signals or barrier semaphores. Data moves between devices by JAX's collectives and lax.ppermute only.
A program may use at most 64 MiB of HBM per device.

v0:
```python
import functools

import jax
import jax.numpy as jnp
from jax import lax
from jax.experimental import pallas as pl
from jax.experimental.pallas import tpu as pltpu
from jax.sharding import PartitionSpec as P

OFF_Y = 8
TAP_ROWS = (0, -4, -3, -2, -1, 1, 2, 3, 4, 0, 0, 0, 0)
TAP_COLS = (0, 0, 0, 0, 0, 0, 0, 0, 0, -2, -1, 1, 2)
PAD = 8
SUB = 8
CHUNK = 8
REACH_ROWS = 4
STEPS = (-2, -1, 1, 2)
PARTS = 2
VMEM = pl.BlockSpec(memory_space=pltpu.VMEM)


def bits_of(count):
    return [1 << k for k in reversed(range(count.bit_length() - 1))]


def reversed_bits(value, count):
    width = count.bit_length() - 1
    total = 0
    for k in range(width):
        total = total + (((value >> k) & 1) << (width - 1 - k))
    return total


def odd_bits(value, count):
    width = count.bit_length() - 1
    total = 0
    for k in range(width):
        total = total ^ ((value >> k) & 1)
    return total


def hop(block, depth_bit, line_bit):
    depths, lines = lax.axis_size("depth"), lax.axis_size("xline")
    route = [
        (d * lines + x, (d ^ depth_bit) * lines + (x ^ line_bit))
        for d in range(depths)
        for x in range(lines)
    ]
    return lax.ppermute(block, ("depth", "xline"), route)


def load_kernel(bins, bins_out):
    bins_out[...] = bins[...]


def clear_edges(buffer):
    count, rows, width = buffer.shape
    zeros = jnp.zeros((PAD, width), jnp.float32)
    for array in range(count):
        buffer[array, 0:PAD, :] = zeros
        buffer[array, rows - PAD : rows, :] = zeros


def build_shifts(shifts, width):
    source = lax.broadcasted_iota(jnp.int32, (width, width), 0)
    target = lax.broadcasted_iota(jnp.int32, (width, width), 1)
    for k, step in enumerate(STEPS):
        matrix = (source == target + step).astype(jnp.bfloat16)
        for part in range(PARTS):
            shifts[part * width : (part + 1) * width, k * width : (k + 1) * width] = matrix


def shift_inline(value, shifts):
    largest = float(jnp.finfo(jnp.bfloat16).max)
    parts = []
    rest = value
    for part in range(PARTS):
        piece = (jnp.clip(rest, -largest, largest) if part == 0 else rest).astype(jnp.bfloat16)
        parts.append(piece)
        if part < PARTS - 1:
            rest = rest - piece.astype(jnp.float32)
    whole = jnp.concatenate(parts, axis=1)
    return jnp.dot(whole, shifts[...], preferred_element_type=jnp.float32)


def run_blocks(sizes, refs, slab, level_index, source, target, first_block, blocks):
    depth_count, line_count, _, row_count, freqs = sizes
    wide, shifts, bins_own, bins_other, shifted = refs
    line_index = lax.axis_index("xline")
    width = wide.shape[2]
    near_count = line_count // 2
    apart = slab ^ lax.axis_index("depth")
    slot = reversed_bits(apart, depth_count)
    odd = odd_bits(apart, depth_count)
    lane = lax.broadcasted_iota(jnp.int32, (SUB, width), 1)
    inside = {
        step: (lane + step >= 0) & (lane + step < width)
        for step in sorted(set(TAP_COLS) - {0} - set(STEPS))
    }
    top = pl.multiple_of(PAD + first_block * SUB, SUB)
    count = blocks * SUB
    rows = [source[array, pl.ds(top, count), :] for array in range(4 * freqs)]
    moved = shift_inline(jnp.concatenate(rows, axis=0), shifts)
    for array in range(4 * freqs):
        shifted[array, 0:count, :] = moved[array * count : (array + 1) * count]
    for block in range(blocks):
        row = pl.multiple_of((first_block + block) * SUB, SUB)
        line = (row // row_count) ^ line_index
        near = reversed_bits(line >> 1, near_count)
        inner = pl.multiple_of(row % row_count, SUB)
        own = bins_own[near, slot, level_index, pl.ds(inner, SUB), :]
        other = bins_other[near, slot, level_index, pl.ds(inner, SUB), :]
        crossed = odd ^ odd_bits(line >> 1, near_count)
        bins = jnp.where((line & 1) == crossed, own, other)
        for freq in range(freqs):
            sums = [None] * 4
            centre = None
            for tap in range(len(TAP_ROWS)):
                coefs = [
                    jnp.take_along_axis(
                        wide[(tap * 2 + part) * freqs + freq],
                        bins,
                        axis=1,
                        mode="promise_in_bounds",
                    )
                    for part in range(2)
                ]
                step = TAP_COLS[tap]
                if step == 0:
                    fields = [
                        source[kind * freqs + freq, pl.ds(PAD + row + TAP_ROWS[tap], SUB), :]
                        for kind in range(4)
                    ]
                    if tap == 0:
                        centre = fields
                elif step in STEPS:
                    lanes = pl.ds(STEPS.index(step) * width, width)
                    fields = [
                        shifted[kind * freqs + freq, pl.ds(block * SUB, SUB), lanes]
                        for kind in range(4)
                    ]
                else:
                    fields = [
                        jnp.where(inside[step], pltpu.roll(value, (-step) % width, 1), 0.0)
                        for value in centre
                    ]
                for field in range(2):
                    real, imag = fields[2 * field], fields[2 * field + 1]
                    term_real = coefs[0] * real - coefs[1] * imag
                    term_imag = coefs[0] * imag + coefs[1] * real
                    for part, term in ((0, term_real), (1, term_imag)):
                        place = 2 * field + part
                        sums[place] = term if sums[place] is None else sums[place] + term
            for kind in range(4):
                target[kind * freqs + freq, pl.ds(PAD + row, SUB), :] = sums[kind]


def run_slab(sizes, refs, slab, first, second, later=None):
    _, line_count, levels, row_count, _ = sizes
    grid_blocks = line_count * row_count // SUB
    chip_blocks = -(-2 * row_count // SUB)
    buffers = (first, second)
    for k in range(levels):
        run = functools.partial(
            run_blocks, sizes, refs, slab, k, buffers[k % 2], buffers[1 - k % 2]
        )
        blocks = grid_blocks
        first_block = 0
        if later is not None:
            reach = OFF_Y + REACH_ROWS * ((later + 1) * levels - 1 - k)
            margin = -(-reach // SUB)
            sides = 1 if line_count == 4 else 2
            blocks = min(grid_blocks, chip_blocks + sides * margin)
            chip = lax.axis_index("xline") >> 1
            first_block = jnp.clip(chip * chip_blocks - margin, 0, grid_blocks - blocks)

        def chunk_step(chunk, carry, run=run, first_block=first_block):
            run(first_block + chunk * CHUNK, CHUNK)
            return carry

        if blocks <= CHUNK:
            run(first_block, blocks)
        else:
            lax.fori_loop(0, blocks // CHUNK, chunk_step, 0)
            if blocks % CHUNK:
                run(first_block + blocks - blocks % CHUNK, blocks % CHUNK)
    if levels % 2:
        first[...] = second[...]


def continuation_kernel(
    sizes,
    table,
    offsets,
    surf_own,
    surf_other,
    bins_own,
    bins_other,
    mine,
    theirs,
    offsets_out,
    wide,
    shifts,
    shifted,
    first,
    second,
):
    _, line_count, _, row_count, freqs = sizes
    depth_index = lax.axis_index("depth")
    line_index = lax.axis_index("xline")
    near_count = line_count // 2
    parity = line_index & 1
    offsets_out[...] = offsets[...]
    for tap in range(len(TAP_ROWS)):
        for part in range(2):
            for freq in range(freqs):
                row = table[tap, part, pl.ds(parity * freqs + freq, 1), :]
                wide[(tap * 2 + part) * freqs + freq] = jnp.broadcast_to(row, wide.shape[1:])
    build_shifts(shifts, wide.shape[2])
    clear_edges(first)
    clear_edges(second)
    for near in range(near_count):
        odd = near.bit_count() & 1
        for own, source in ((odd, surf_own), (1 - odd, surf_other)):
            line = line_index ^ (2 * reversed_bits(near, near_count) + own)
            start = pl.multiple_of(PAD + line * row_count, SUB)
            for kind in range(4):
                for freq in range(freqs):
                    block = source[near, kind, parity * freqs + freq]
                    if kind == 3:
                        block = -block
                    first[kind * freqs + freq, pl.ds(start, row_count), :] = block
    refs = (wide, shifts, bins_own, bins_other, shifted)

    def slab_step(slab, carry, later=None):
        run_slab(sizes, refs, slab, first, second, later)
        return carry

    before_last = jnp.maximum(depth_index - 1, 0)
    lax.fori_loop(0, before_last, slab_step, 0)
    lax.fori_loop(before_last, depth_index, functools.partial(slab_step, later=1), 0)
    slab_step(depth_index, 0, later=0)
    tall = row_count + 2 * OFF_Y
    for out, line in ((mine, line_index), (theirs, line_index ^ 1)):
        base = pl.multiple_of(PAD + line * row_count, SUB)
        for array in range(2 * freqs):
            out[array * row_count : (array + 1) * row_count, :] = first[
                array, pl.ds(base, row_count), :
            ]
            below = 2 * freqs * row_count + array * tall
            above = pl.multiple_of(base - OFF_Y, SUB)
            out[below : below + tall, :] = first[2 * freqs + array, pl.ds(above, tall), :]


def image_kernel(freqs, offsets, mine, other, image):
    row_count, width = image.shape[2:]
    tall = row_count + 2 * OFF_Y
    lanes = lax.broadcasted_iota(jnp.int32, (row_count, width), 1)
    for h in range(image.shape[1]):
        dy = offsets[0, h]
        dx = offsets[1, h]
        valid = (lanes + dx >= 0) & (lanes + dx < width)
        total = None
        for pack in (mine, other):
            for array in range(2 * freqs):
                source = pack[array * row_count : (array + 1) * row_count, :]
                start = 2 * freqs * row_count + array * tall + OFF_Y
                value = pack[pl.ds(start + dy, row_count), :]
                term = source * pltpu.roll(value, lax.rem(width - dx, width), 1)
                if array >= freqs:
                    term = -term
                total = term if total is None else total + term
        image[0, h] = jnp.where(valid, total, 0.0)


def shards(surface_fields, stencil_table, velocity_bins, offset_list):
    depth_count = lax.axis_size("depth")
    line_count = lax.axis_size("xline")
    row_count = surface_fields.shape[3]
    width = surface_fields.shape[4]
    freqs = surface_fields.shape[2] // 2
    levels = velocity_bins.shape[1]
    grid_rows = row_count * line_count
    sizes = (depth_count, line_count, levels, row_count, freqs)
    depth_bits = bits_of(depth_count)
    line_bits = bits_of(line_count)[:-1]
    f32 = jnp.float32

    def call(kernel, outs, scratch, flops, *args):
        size = sum(array.size for array in (*args, *outs, *scratch))
        return pl.pallas_call(
            kernel,
            out_shape=outs,
            in_specs=[VMEM] * len(args),
            out_specs=[VMEM] * len(outs),
            scratch_shapes=[pltpu.VMEM(array.shape, array.dtype) for array in scratch],
            compiler_params=pltpu.CompilerParams(vmem_limit_bytes=4 * size + (2 << 20)),
            cost_estimate=pl.CostEstimate(flops=flops, bytes_accessed=4 * size, transcendentals=0),
        )(*args)

    like = jax.ShapeDtypeStruct
    surf = surface_fields.reshape(1, 4, 2 * freqs, row_count, width)
    (bins,) = call(
        load_kernel, [like(velocity_bins.shape, velocity_bins.dtype)], [], 1000, velocity_bins
    )

    top, below = depth_bits[:2]
    last, line = depth_bits[-1], line_bits[0]
    parts = [velocity_bins] + [
        hop(velocity_bins, bit, bit.bit_count() & 1)
        for bit in (top, top | below, below)
    ]
    parts[0] = bins
    bins = jnp.concatenate([parts[0], parts[1], parts[3], parts[2]], axis=0)
    surf = jnp.concatenate([surf, hop(surf, 0, line | 1)], axis=0)
    for bit in depth_bits[2:-1]:
        bins = jnp.concatenate([bins, hop(bins, bit, 1)], axis=0)
    depth_part = hop(bins, last, 1)
    line_part = hop(bins, 0, line | 1)
    cross_part = hop(bins, last, line)
    bins = jnp.stack(
        [
            jnp.concatenate([bins, depth_part], axis=0),
            jnp.concatenate([line_part, cross_part], axis=0),
        ]
    )
    for bit in line_bits[1:]:
        bins = jnp.concatenate([bins, hop(bins, 0, bit | 1)], axis=0)
        surf = jnp.concatenate([surf, hop(surf, 0, bit | 1)], axis=0)
    surf_other = hop(surf, 0, 1)
    bins_other = hop(bins, 0, 1)

    field_shape = (4 * freqs, grid_rows + 2 * PAD, width)
    field = like(field_shape, f32)
    work = depth_count * levels * len(TAP_ROWS) * 8 * field_shape[0] * grid_rows * width
    pack = like((2 * freqs * (2 * row_count + 2 * OFF_Y), width), f32)
    offsets = offset_list.T
    mine, theirs, offsets = call(
        functools.partial(continuation_kernel, sizes),
        [pack, pack, like(offsets.shape, offsets.dtype)],
        [
            like((len(TAP_ROWS) * 2 * freqs, SUB, width), f32),
            like((PARTS * width, len(STEPS) * width), jnp.bfloat16),
            like((4 * freqs, CHUNK * SUB, len(STEPS) * width), f32),
            field,
            field,
        ],
        work,
        stencil_table,
        offsets,
        surf,
        surf_other,
        bins,
        bins_other,
    )
    other = hop(theirs, 0, 1)
    image = pl.pallas_call(
        functools.partial(image_kernel, freqs),
        out_shape=like((1, offset_list.shape[0], row_count, width), f32),
        in_specs=[VMEM, VMEM, VMEM],
        out_specs=VMEM,
        compiler_params=pltpu.CompilerParams(vmem_limit_bytes=4 << 20),
        name="imaging",
    )(offsets, mine, other)
    return image


def solution(mesh):
    return jax.shard_map(
        shards,
        mesh=mesh,
        in_specs=(P(None, None, None, "xline", None), P(), P("depth", None, "xline", None), P()),
        out_specs=P("depth", None, "xline", None),
        check_vma=False,
    )
```

profile of v0, /device:TPU:29, one launch (start us, length us, event | category | flops | bytes accessed | tf_op | source)
XLA Modules:
  0.0 22.9 jit_solution(14742860911935809439)
XLA Ops:
  0.0 0.6 %collective-permute-start.2 = (s32[1,2,16,128]{3,2,1,0:T(8,128)}, s32[1,2,16,128]{3,2,1,0:T(8,128)S(1)}, u32[]{:S(2)}, u32[]{:S(2)}) collective-permute-start(s32[1,2,16,128]{3,2,1,0:T(8,128)} %bins.1), channel_id=1, source_target_pairs={{0,17},{1,16},{2,19},{3,18},{4,21},{5,20},{6,23},{7,22},{8,25},{9,... | collective-permute-start | bytes 49160 | tf_op jit(solution)/shard_map/ppermute | solution.py:49
  0.6 2.2 %collective-permute-start.4 = (s32[1,2,16,128]{3,2,1,0:T(8,128)}, s32[1,2,16,128]{3,2,1,0:T(8,128)S(1)}, u32[]{:S(2)}, u32[]{:S(2)}) collective-permute-start(s32[1,2,16,128]{3,2,1,0:T(8,128)} %bins.1), channel_id=1, source_target_pairs={{0,24},{1,25},{2,26},{3,27},{4,28},{5,29},{6,30},{7,31},{8,16},{9,... | collective-permute-start | bytes 49160 | tf_op jit(solution)/shard_map/ppermute | solution.py:49
  2.8 0.4 %collective-permute-start.3 = (s32[1,2,16,128]{3,2,1,0:T(8,128)}, s32[1,2,16,128]{3,2,1,0:T(8,128)S(1)}, u32[]{:S(2)}, u32[]{:S(2)}) collective-permute-start(s32[1,2,16,128]{3,2,1,0:T(8,128)} %bins.1), channel_id=1, source_target_pairs={{0,9},{1,8},{2,11},{3,10},{4,13},{5,12},{6,15},{7,14},{8,1},{9,0},... | collective-permute-start | bytes 49160 | tf_op jit(solution)/shard_map/ppermute | solution.py:49
  3.2 1.5 %collective-permute-start = (f32[1,4,2,16,128]{4,3,2,1,0:T(8,128)}, f32[1,4,2,16,128]{4,3,2,1,0:T(8,128)S(1)}, u32[]{:S(2)}, u32[]{:S(2)}) collective-permute-start(f32[1,4,2,16,128]{4,3,2,1,0:T(8,128)} %bitcast.7), channel_id=1, source_target_pairs={{0,3},{1,2},{2,1},{3,0},{4,7},{5,6},{6,5},{7,4},{8,11},{9,10},{10,... | collective-permute-start | bytes 196616 | tf_op jit(solution)/shard_map/ppermute | solution.py:49
  4.7 0.0 copy-start.1
  4.7 0.7 %copy-done.1 = s32[1,2,16,128]{3,2,1,0:T(8,128)S(1)} copy-done((s32[1,2,16,128]{3,2,1,0:T(8,128)S(1)}, s32[1,2,16,128]{3,2,1,0:T(8,128)}, u32[]{:S(2)}) %copy-start.1) | copy-done | bytes 16408
  5.4 0.0 collective-permute-done.2
  5.4 0.0 collective-permute-done.4
  5.4 1.0 %collective-permute-done.3 = s32[1,2,16,128]{3,2,1,0:T(8,128)S(1)} collective-permute-done((s32[1,2,16,128]{3,2,1,0:T(8,128)}, s32[1,2,16,128]{3,2,1,0:T(8,128)S(1)}, u32[]{:S(2)}, u32[]{:S(2)}) %collective-permute-start.3) | collective-permute-done | bytes 16416 | tf_op jit(solution)/shard_map/ppermute | solution.py:49
  6.5 1.2 %collective-permute-start.7 = (s32[4,2,16,128]{3,2,1,0:T(8,128)S(1)}, s32[4,2,16,128]{3,2,1,0:T(8,128)S(1)}, u32[]{:S(2)}, u32[]{:S(2)}) collective-permute-start(s32[4,2,16,128]{3,2,1,0:T(8,128)S(1)} %pad_add_fusion.1), channel_id=1, source_target_pairs={{0,6},{1,7},{2,4},{3,5},{4,2},{5,3},{6,0},{7,1},{8,14},{9,15},{10,... | collective-permute-start | bytes 196616 | tf_op jit(solution)/shard_map/ppermute | solution.py:49
  7.6 0.5 %collective-permute-start.6 = (s32[4,2,16,128]{3,2,1,0:T(8,128)S(1)}, s32[4,2,16,128]{3,2,1,0:T(8,128)S(1)}, u32[]{:S(2)}, u32[]{:S(2)}) collective-permute-start(s32[4,2,16,128]{3,2,1,0:T(8,128)S(1)} %pad_add_fusion.1), channel_id=1, source_target_pairs={{0,3},{1,2},{2,1},{3,0},{4,7},{5,6},{6,5},{7,4},{8,11},{9,10},{10,... | collective-permute-start | bytes 196616 | tf_op jit(solution)/shard_map/ppermute | solution.py:49
  8.1 1.3 %collective-permute-start.5 = (s32[4,2,16,128]{3,2,1,0:T(8,128)S(1)}, s32[4,2,16,128]{3,2,1,0:T(8,128)S(1)}, u32[]{:S(2)}, u32[]{:S(2)}) collective-permute-start(s32[4,2,16,128]{3,2,1,0:T(8,128)S(1)} %pad_add_fusion.1), channel_id=1, source_target_pairs={{0,5},{1,4},{2,7},{3,6},{4,1},{5,0},{6,3},{7,2},{8,13},{9,12},{10,... | collective-permute-start | bytes 196616 | tf_op jit(solution)/shard_map/ppermute | solution.py:49
  9.4 1.5 %collective-permute-done.7 = s32[4,2,16,128]{3,2,1,0:T(8,128)S(1)} collective-permute-done((s32[4,2,16,128]{3,2,1,0:T(8,128)S(1)}, s32[4,2,16,128]{3,2,1,0:T(8,128)S(1)}, u32[]{:S(2)}, u32[]{:S(2)}) %collective-permute-start.7) | collective-permute-done | bytes 65568 | tf_op jit(solution)/shard_map/ppermute | solution.py:49
  11.0 1.0 %collective-permute-done.6 = s32[4,2,16,128]{3,2,1,0:T(8,128)S(1)} collective-permute-done((s32[4,2,16,128]{3,2,1,0:T(8,128)S(1)}, s32[4,2,16,128]{3,2,1,0:T(8,128)S(1)}, u32[]{:S(2)}, u32[]{:S(2)}) %collective-permute-start.6) | collective-permute-done | bytes 65568 | tf_op jit(solution)/shard_map/ppermute | solution.py:49
  12.0 0.9 %collective-permute-done.5 = s32[4,2,16,128]{3,2,1,0:T(8,128)S(1)} collective-permute-done((s32[4,2,16,128]{3,2,1,0:T(8,128)S(1)}, s32[4,2,16,128]{3,2,1,0:T(8,128)S(1)}, u32[]{:S(2)}, u32[]{:S(2)}) %collective-permute-start.5) | collective-permute-done | bytes 65568 | tf_op jit(solution)/shard_map/ppermute | solution.py:49
  12.9 0.0 copy-start.3
  12.9 0.0 copy-start
  12.9 0.5 %collective-permute-start.8 = (s32[2,8,2,16,128]{4,3,2,1,0:T(8,128)S(1)}, s32[2,8,2,16,128]{4,3,2,1,0:T(8,128)S(1)}, u32[]{:S(2)}, u32[]{:S(2)}) collective-permute-start(s32[2,8,2,16,128]{4,3,2,1,0:T(8,128)S(1)} %pad_add_fusion.bins_own), channel_id=1, source_target_pairs={{0,1},{1,0},{2,3},{3,2},{4,5},{5,4},{6,7},{7,6},{8,9},{9,8},{10,11... | collective-permute-start | bytes 786440 | tf_op jit(solution)/shard_map/ppermute | solution.py:49
  13.4 0.0 collective-permute-done
  13.4 0.3 %copy-done.3 = f32[2,2,2,16,128]{4,3,2,1,0:T(8,128)S(1)} copy-done((f32[2,2,2,16,128]{4,3,2,1,0:T(8,128)S(1)}, f32[2,2,2,16,128]{4,3,2,1,0:T(8,128)}, u32[]{:S(2)}) %copy-start.3) | copy-done | bytes 65560
  13.7 0.0 copy-start.2
  13.7 0.5 %collective-permute-start.1 = (f32[2,4,2,16,128]{4,3,2,1,0:T(8,128)S(1)}, f32[2,4,2,16,128]{4,3,2,1,0:T(8,128)S(1)}, u32[]{:S(2)}, u32[]{:S(2)}) collective-permute-start(f32[2,4,2,16,128]{4,3,2,1,0:T(8,128)S(1)} %pad_maximum_fusion.surf_own), channel_id=1, source_target_pairs={{0,1},{1,0},{2,3},{3,2},{4,5},{5,4},{6,7},{7,6},{8,9},{9,8},{10,11... | collective-permute-start | bytes 393224 | tf_op jit(solution)/shard_map/ppermute | solution.py:49
  14.2 1.0 %collective-permute-done.1.surf_other = f32[2,4,2,16,128]{4,3,2,1,0:T(8,128)S(1)} collective-permute-done((f32[2,4,2,16,128]{4,3,2,1,0:T(8,128)S(1)}, f32[2,4,2,16,128]{4,3,2,1,0:T(8,128)S(1)}, u32[]{:S(2)}, u32[]{:S(2)}) %collective-permute-start.1) | collective-permute-done | bytes 131104 | tf_op jit(solution)/shard_map/ppermute | solution.py:49
  15.2 0.0 collective-permute-done.8.bins_other
  15.2 0.0 copy-done
  15.2 0.0 copy-done.2
  15.2 5.4 %shard_map.47 = (f32[96,128]{1,0:T(8,128)S(1)}, f32[96,128]{1,0:T(8,128)S(1)}, s32[2,16]{1,0:T(2,128)S(1)}) custom-call(f32[13,2,2,128]{3,2,1,0:T(2,128)S(1)} %copy-done, s32[2,16]{1,0:T(2,128)S(1)} %bitcast.5, f32[2,4,2,16,128]{4,3,2,1,0:T(8,128)S(1)} %pad_maximum_fusion.surf_own, f32[2,4,2,16,128]{4,3,2,1,0:T(8,128)S(1)} %collective-permute-done.1.surf_other, ...), custom_call_target="tpu_custom_call" | custom-call | flops 54525952 | bytes 2394368 | tf_op jit(solution)/shard_map/pallas_call | solution.py:291
  20.6 0.4 %collective-permute-start.9 = (f32[96,128]{1,0:T(8,128)S(1)}, f32[96,128]{1,0:T(8,128)S(1)}, u32[]{:S(2)}, u32[]{:S(2)}) collective-permute-start(f32[96,128]{1,0:T(8,128)S(1)} %get-tuple-element.10), channel_id=1, source_target_pairs={{0,1},{1,0},{2,3},{3,2},{4,5},{5,4},{6,7},{7,6},{8,9},{9,8},{10,11... | collective-permute-start | bytes 147464 | tf_op jit(solution)/shard_map/ppermute | solution.py:49
  21.0 0.9 %collective-permute-done.9.other = f32[96,128]{1,0:T(8,128)S(1)} collective-permute-done((f32[96,128]{1,0:T(8,128)S(1)}, f32[96,128]{1,0:T(8,128)S(1)}, u32[]{:S(2)}, u32[]{:S(2)}) %collective-permute-start.9) | collective-permute-done | bytes 49184 | tf_op jit(solution)/shard_map/ppermute | solution.py:49
  21.9 1.0 %imaging.1 = f32[1,16,16,128]{3,2,1,0:T(8,128)} custom-call(s32[2,16]{1,0:T(2,128)S(1)} %get-tuple-element.8.offsets, f32[96,128]{1,0:T(8,128)S(1)} %get-tuple-element.9.mine, f32[96,128]{1,0:T(8,128)S(1)} %collective-permute-done.9.other), custom_call_target="tpu_custom_call" | custom-call | tf_op jit(solution)/shard_map/imaging/pallas_call | solution.py:357
  (10 shorter events, 0.1 us)
Async XLA Ops:
  0.0 5.4 %collective-permute-start.2 = (s32[1,2,16,128]{3,2,1,0:T(8,128)}, s32[1,2,16,128]{3,2,1,0:T(8,128)S(1)}, u32[]{:S(2)}, u32[]{:S(2)}) collective-permute-start(s32[1,2,16,128]{3,2,1,0:T(8,128)} %bins.1), channel_id=1, source_target_pairs={{0,17},{1,16},{2,19},{3,18},{4,21},{5,20},{6,23},{7,22},{8,25},{9,... | collective-permute-start | bytes 49160 | tf_op jit(solution)/shard_map/ppermute | solution.py:49
  0.6 4.8 %collective-permute-start.4 = (s32[1,2,16,128]{3,2,1,0:T(8,128)}, s32[1,2,16,128]{3,2,1,0:T(8,128)S(1)}, u32[]{:S(2)}, u32[]{:S(2)}) collective-permute-start(s32[1,2,16,128]{3,2,1,0:T(8,128)} %bins.1), channel_id=1, source_target_pairs={{0,24},{1,25},{2,26},{3,27},{4,28},{5,29},{6,30},{7,31},{8,16},{9,... | collective-permute-start | bytes 49160 | tf_op jit(solution)/shard_map/ppermute | solution.py:49
  2.8 3.7 %collective-permute-start.3 = (s32[1,2,16,128]{3,2,1,0:T(8,128)}, s32[1,2,16,128]{3,2,1,0:T(8,128)S(1)}, u32[]{:S(2)}, u32[]{:S(2)}) collective-permute-start(s32[1,2,16,128]{3,2,1,0:T(8,128)} %bins.1), channel_id=1, source_target_pairs={{0,9},{1,8},{2,11},{3,10},{4,13},{5,12},{6,15},{7,14},{8,1},{9,0},... | collective-permute-start | bytes 49160 | tf_op jit(solution)/shard_map/ppermute | solution.py:49
  3.2 10.2 %collective-permute-start = (f32[1,4,2,16,128]{4,3,2,1,0:T(8,128)}, f32[1,4,2,16,128]{4,3,2,1,0:T(8,128)S(1)}, u32[]{:S(2)}, u32[]{:S(2)}) collective-permute-start(f32[1,4,2,16,128]{4,3,2,1,0:T(8,128)} %bitcast.7), channel_id=1, source_target_pairs={{0,3},{1,2},{2,1},{3,0},{4,7},{5,6},{6,5},{7,4},{8,11},{9,10},{10,... | collective-permute-start | bytes 196616 | tf_op jit(solution)/shard_map/ppermute | solution.py:49
  4.7 0.7 %copy-start.1 = (s32[1,2,16,128]{3,2,1,0:T(8,128)S(1)}, s32[1,2,16,128]{3,2,1,0:T(8,128)}, u32[]{:S(2)}) copy-start(s32[1,2,16,128]{3,2,1,0:T(8,128)} %bins.1) | copy-start | bytes 49156
  6.5 4.5 %collective-permute-start.7 = (s32[4,2,16,128]{3,2,1,0:T(8,128)S(1)}, s32[4,2,16,128]{3,2,1,0:T(8,128)S(1)}, u32[]{:S(2)}, u32[]{:S(2)}) collective-permute-start(s32[4,2,16,128]{3,2,1,0:T(8,128)S(1)} %pad_add_fusion.1), channel_id=1, source_target_pairs={{0,6},{1,7},{2,4},{3,5},{4,2},{5,3},{6,0},{7,1},{8,14},{9,15},{10,... | collective-permute-start | bytes 196616 | tf_op jit(solution)/shard_map/ppermute | solution.py:49
  7.6 4.3 %collective-permute-start.6 = (s32[4,2,16,128]{3,2,1,0:T(8,128)S(1)}, s32[4,2,16,128]{3,2,1,0:T(8,128)S(1)}, u32[]{:S(2)}, u32[]{:S(2)}) collective-permute-start(s32[4,2,16,128]{3,2,1,0:T(8,128)S(1)} %pad_add_fusion.1), channel_id=1, source_target_pairs={{0,3},{1,2},{2,1},{3,0},{4,7},{5,6},{6,5},{7,4},{8,11},{9,10},{10,... | collective-permute-start | bytes 196616 | tf_op jit(solution)/shard_map/ppermute | solution.py:49
  8.1 4.7 %collective-permute-start.5 = (s32[4,2,16,128]{3,2,1,0:T(8,128)S(1)}, s32[4,2,16,128]{3,2,1,0:T(8,128)S(1)}, u32[]{:S(2)}, u32[]{:S(2)}) collective-permute-start(s32[4,2,16,128]{3,2,1,0:T(8,128)S(1)} %pad_add_fusion.1), channel_id=1, source_target_pairs={{0,5},{1,4},{2,7},{3,6},{4,1},{5,0},{6,3},{7,2},{8,13},{9,12},{10,... | collective-permute-start | bytes 196616 | tf_op jit(solution)/shard_map/ppermute | solution.py:49
  12.9 0.8 %copy-start.3 = (f32[2,2,2,16,128]{4,3,2,1,0:T(8,128)S(1)}, f32[2,2,2,16,128]{4,3,2,1,0:T(8,128)}, u32[]{:S(2)}) copy-start(f32[2,2,2,16,128]{4,3,2,1,0:T(8,128)} %param.4) | copy-start | bytes 196612
  12.9 2.3 %copy-start = (f32[13,2,2,128]{3,2,1,0:T(2,128)S(1)}, f32[13,2,2,128]{3,2,1,0:T(2,128)}, u32[]{:S(2)}) copy-start(f32[13,2,2,128]{3,2,1,0:T(2,128)} %table.1) | copy-start | bytes 79876
  12.9 2.3 %collective-permute-start.8 = (s32[2,8,2,16,128]{4,3,2,1,0:T(8,128)S(1)}, s32[2,8,2,16,128]{4,3,2,1,0:T(8,128)S(1)}, u32[]{:S(2)}, u32[]{:S(2)}) collective-permute-start(s32[2,8,2,16,128]{4,3,2,1,0:T(8,128)S(1)} %pad_add_fusion.bins_own), channel_id=1, source_target_pairs={{0,1},{1,0},{2,3},{3,2},{4,5},{5,4},{6,7},{7,6},{8,9},{9,8},{10,11... | collective-permute-start | bytes 786440 | tf_op jit(solution)/shard_map/ppermute | solution.py:49
  13.7 1.5 %copy-start.2 = (s32[16,2]{0,1:T(2,128)S(1)}, s32[16,2]{0,1:T(2,128)}, u32[]{:S(2)}) copy-start(s32[16,2]{0,1:T(2,128)} %param.7) | copy-start | bytes 388
  13.7 1.4 %collective-permute-start.1 = (f32[2,4,2,16,128]{4,3,2,1,0:T(8,128)S(1)}, f32[2,4,2,16,128]{4,3,2,1,0:T(8,128)S(1)}, u32[]{:S(2)}, u32[]{:S(2)}) collective-permute-start(f32[2,4,2,16,128]{4,3,2,1,0:T(8,128)S(1)} %pad_maximum_fusion.surf_own), channel_id=1, source_target_pairs={{0,1},{1,0},{2,3},{3,2},{4,5},{5,4},{6,7},{7,6},{8,9},{9,8},{10,11... | collective-permute-start | bytes 393224 | tf_op jit(solution)/shard_map/ppermute | solution.py:49
  20.6 1.3 %collective-permute-start.9 = (f32[96,128]{1,0:T(8,128)S(1)}, f32[96,128]{1,0:T(8,128)S(1)}, u32[]{:S(2)}, u32[]{:S(2)}) collective-permute-start(f32[96,128]{1,0:T(8,128)S(1)} %get-tuple-element.10), channel_id=1, source_target_pairs={{0,1},{1,0},{2,3},{3,2},{4,5},{5,4},{6,7},{7,6},{8,9},{9,8},{10,11... | collective-permute-start | bytes 147464 | tf_op jit(solution)/shard_map/ppermute | solution.py:49
where the time goes:
time: 23.1 us; the launch traced here: 22.9 us
  starting transfers between devices  8.98 us (39%)
  Pallas kernels  6.39 us (28%)
  waiting for transfers between devices  6.33 us (27%)
  local copies, waits for them, and re-layouts  1.08 us (5%)
    ppermute x10, starting transfers between devices, hop(): return lax.ppermute(block, ('depth', 'xline'), route)  8.98 us
    ppermute x10, waiting for transfers between devices, hop(): return lax.ppermute(block, ('depth', 'xline'), route)  6.33 us
    pallas_call x2, Pallas kernels, call(): pl.pallas_call(kernel, out_shape=outs, in_specs=[VMEM] * len(args), out_s...  5.44 us
    unnamed x12, local copies, waits for them, and re-layouts  1.08 us
    pallas_call x1, Pallas kernels, shards(): pl.pallas_call(functools.partial(image_kernel, freqs), out_shape=like((1,...  0.96 us
  transfers between devices with their start and end apart: 10, of which 6 were waited for; matrix products, arithmetic and copies ran while one was open for 0% of the time, Pallas kernels for 0%

commit v1 on v0

--- a/solution.py
+++ b/solution.py
@@ -99,10 +99,13 @@
     }
     top = pl.multiple_of(PAD + first_block * SUB, SUB)
     count = blocks * SUB
-    rows = [source[array, pl.ds(top, count), :] for array in range(4 * freqs)]
-    moved = shift_inline(jnp.concatenate(rows, axis=0), shifts)
-    for array in range(4 * freqs):
-        shifted[array, 0:count, :] = moved[array * count : (array + 1) * count]
+    half = (blocks + 1) // 2 * SUB
+    for low, high in ((0, half), (half, count)):
+        size = high - low
+        rows = [source[array, pl.ds(top + low, size), :] for array in range(4 * freqs)]
+        moved = shift_inline(jnp.concatenate(rows, axis=0), shifts)
+        for array in range(4 * freqs):
+            shifted[array, low:high, :] = moved[array * size : (array + 1) * size]
     for block in range(blocks):
         row = pl.multiple_of((first_block + block) * SUB, SUB)
         line = (row // row_count) ^ line_index

time: 23.1 us -> 22.9 us (level)
  no operation moved by 1% of the time
where the time goes in v1:
time: 22.9 us; the launch traced here: 22.7 us
  starting transfers between devices  8.98 us (39%)
  waiting for transfers between devices  6.33 us (28%)
  Pallas kernels  6.16 us (27%)
  local copies, waits for them, and re-layouts  1.08 us (5%)
    ppermute x10, starting transfers between devices, hop(): return lax.ppermute(block, ('depth', 'xline'), route)  8.98 us
    ppermute x10, waiting for transfers between devices, hop(): return lax.ppermute(block, ('depth', 'xline'), route)  6.33 us
    pallas_call x2, Pallas kernels, call(): pl.pallas_call(kernel, out_shape=outs, in_specs=[VMEM] * len(args), out_s...  5.21 us
    unnamed x12, local copies, waits for them, and re-layouts  1.08 us
    pallas_call x1, Pallas kernels, shards(): pl.pallas_call(functools.partial(image_kernel, freqs), out_shape=like((1,...  0.96 us
  transfers between devices with their start and end apart: 10, of which 6 were waited for; matrix products, arithmetic and copies ran while one was open for 0% of the time, Pallas kernels for 0%

profile of v1, /device:TPU:29, one launch (start us, length us, event | category | flops | bytes accessed | tf_op | source)
XLA Modules:
  0.0 22.7 jit_solution(2378120352090186036)
XLA Ops:
  0.0 0.6 %collective-permute-start.2 = (s32[1,2,16,128]{3,2,1,0:T(8,128)}, s32[1,2,16,128]{3,2,1,0:T(8,128)S(1)}, u32[]{:S(2)}, u32[]{:S(2)}) collective-permute-start(s32[1,2,16,128]{3,2,1,0:T(8,128)} %bins.1), channel_id=1, source_target_pairs={{0,17},{1,16},{2,19},{3,18},{4,21},{5,20},{6,23},{7,22},{8,25},{9,... | collective-permute-start | bytes 49160 | tf_op jit(solution)/shard_map/ppermute | solution.py:49
  0.6 2.2 %collective-permute-start.4 = (s32[1,2,16,128]{3,2,1,0:T(8,128)}, s32[1,2,16,128]{3,2,1,0:T(8,128)S(1)}, u32[]{:S(2)}, u32[]{:S(2)}) collective-permute-start(s32[1,2,16,128]{3,2,1,0:T(8,128)} %bins.1), channel_id=1, source_target_pairs={{0,24},{1,25},{2,26},{3,27},{4,28},{5,29},{6,30},{7,31},{8,16},{9,... | collective-permute-start | bytes 49160 | tf_op jit(solution)/shard_map/ppermute | solution.py:49
  2.8 0.4 %collective-permute-start.3 = (s32[1,2,16,128]{3,2,1,0:T(8,128)}, s32[1,2,16,128]{3,2,1,0:T(8,128)S(1)}, u32[]{:S(2)}, u32[]{:S(2)}) collective-permute-start(s32[1,2,16,128]{3,2,1,0:T(8,128)} %bins.1), channel_id=1, source_target_pairs={{0,9},{1,8},{2,11},{3,10},{4,13},{5,12},{6,15},{7,14},{8,1},{9,0},... | collective-permute-start | bytes 49160 | tf_op jit(solution)/shard_map/ppermute | solution.py:49
  3.2 1.5 %collective-permute-start = (f32[1,4,2,16,128]{4,3,2,1,0:T(8,128)}, f32[1,4,2,16,128]{4,3,2,1,0:T(8,128)S(1)}, u32[]{:S(2)}, u32[]{:S(2)}) collective-permute-start(f32[1,4,2,16,128]{4,3,2,1,0:T(8,128)} %bitcast.7), channel_id=1, source_target_pairs={{0,3},{1,2},{2,1},{3,0},{4,7},{5,6},{6,5},{7,4},{8,11},{9,10},{10,... | collective-permute-start | bytes 196616 | tf_op jit(solution)/shard_map/ppermute | solution.py:49
  4.7 0.0 copy-start.1
  4.7 0.7 %copy-done.1 = s32[1,2,16,128]{3,2,1,0:T(8,128)S(1)} copy-done((s32[1,2,16,128]{3,2,1,0:T(8,128)S(1)}, s32[1,2,16,128]{3,2,1,0:T(8,128)}, u32[]{:S(2)}) %copy-start.1) | copy-done | bytes 16408
  5.4 0.0 collective-permute-done.2
  5.4 0.0 collective-permute-done.4
  5.4 1.0 %collective-permute-done.3 = s32[1,2,16,128]{3,2,1,0:T(8,128)S(1)} collective-permute-done((s32[1,2,16,128]{3,2,1,0:T(8,128)}, s32[1,2,16,128]{3,2,1,0:T(8,128)S(1)}, u32[]{:S(2)}, u32[]{:S(2)}) %collective-permute-start.3) | collective-permute-done | bytes 16416 | tf_op jit(solution)/shard_map/ppermute | solution.py:49
  6.5 1.2 %collective-permute-start.7 = (s32[4,2,16,128]{3,2,1,0:T(8,128)S(1)}, s32[4,2,16,128]{3,2,1,0:T(8,128)S(1)}, u32[]{:S(2)}, u32[]{:S(2)}) collective-permute-start(s32[4,2,16,128]{3,2,1,0:T(8,128)S(1)} %pad_add_fusion.1), channel_id=1, source_target_pairs={{0,6},{1,7},{2,4},{3,5},{4,2},{5,3},{6,0},{7,1},{8,14},{9,15},{10,... | collective-permute-start | bytes 196616 | tf_op jit(solution)/shard_map/ppermute | solution.py:49
  7.6 0.5 %collective-permute-start.6 = (s32[4,2,16,128]{3,2,1,0:T(8,128)S(1)}, s32[4,2,16,128]{3,2,1,0:T(8,128)S(1)}, u32[]{:S(2)}, u32[]{:S(2)}) collective-permute-start(s32[4,2,16,128]{3,2,1,0:T(8,128)S(1)} %pad_add_fusion.1), channel_id=1, source_target_pairs={{0,3},{1,2},{2,1},{3,0},{4,7},{5,6},{6,5},{7,4},{8,11},{9,10},{10,... | collective-permute-start | bytes 196616 | tf_op jit(solution)/shard_map/ppermute | solution.py:49
  8.1 1.3 %collective-permute-start.5 = (s32[4,2,16,128]{3,2,1,0:T(8,128)S(1)}, s32[4,2,16,128]{3,2,1,0:T(8,128)S(1)}, u32[]{:S(2)}, u32[]{:S(2)}) collective-permute-start(s32[4,2,16,128]{3,2,1,0:T(8,128)S(1)} %pad_add_fusion.1), channel_id=1, source_target_pairs={{0,5},{1,4},{2,7},{3,6},{4,1},{5,0},{6,3},{7,2},{8,13},{9,12},{10,... | collective-permute-start | bytes 196616 | tf_op jit(solution)/shard_map/ppermute | solution.py:49
  9.4 1.5 %collective-permute-done.7 = s32[4,2,16,128]{3,2,1,0:T(8,128)S(1)} collective-permute-done((s32[4,2,16,128]{3,2,1,0:T(8,128)S(1)}, s32[4,2,16,128]{3,2,1,0:T(8,128)S(1)}, u32[]{:S(2)}, u32[]{:S(2)}) %collective-permute-start.7) | collective-permute-done | bytes 65568 | tf_op jit(solution)/shard_map/ppermute | solution.py:49
  11.0 1.0 %collective-permute-done.6 = s32[4,2,16,128]{3,2,1,0:T(8,128)S(1)} collective-permute-done((s32[4,2,16,128]{3,2,1,0:T(8,128)S(1)}, s32[4,2,16,128]{3,2,1,0:T(8,128)S(1)}, u32[]{:S(2)}, u32[]{:S(2)}) %collective-permute-start.6) | collective-permute-done | bytes 65568 | tf_op jit(solution)/shard_map/ppermute | solution.py:49
  12.0 0.9 %collective-permute-done.5 = s32[4,2,16,128]{3,2,1,0:T(8,128)S(1)} collective-permute-done((s32[4,2,16,128]{3,2,1,0:T(8,128)S(1)}, s32[4,2,16,128]{3,2,1,0:T(8,128)S(1)}, u32[]{:S(2)}, u32[]{:S(2)}) %collective-permute-start.5) | collective-permute-done | bytes 65568 | tf_op jit(solution)/shard_map/ppermute | solution.py:49
  12.9 0.0 copy-start.3
  12.9 0.0 copy-start
  12.9 0.5 %collective-permute-start.8 = (s32[2,8,2,16,128]{4,3,2,1,0:T(8,128)S(1)}, s32[2,8,2,16,128]{4,3,2,1,0:T(8,128)S(1)}, u32[]{:S(2)}, u32[]{:S(2)}) collective-permute-start(s32[2,8,2,16,128]{4,3,2,1,0:T(8,128)S(1)} %pad_add_fusion.bins_own), channel_id=1, source_target_pairs={{0,1},{1,0},{2,3},{3,2},{4,5},{5,4},{6,7},{7,6},{8,9},{9,8},{10,11... | collective-permute-start | bytes 786440 | tf_op jit(solution)/shard_map/ppermute | solution.py:49
  13.4 0.0 collective-permute-done
  13.4 0.3 %copy-done.3 = f32[2,2,2,16,128]{4,3,2,1,0:T(8,128)S(1)} copy-done((f32[2,2,2,16,128]{4,3,2,1,0:T(8,128)S(1)}, f32[2,2,2,16,128]{4,3,2,1,0:T(8,128)}, u32[]{:S(2)}) %copy-start.3) | copy-done | bytes 65560
  13.7 0.0 copy-start.2
  13.7 0.5 %collective-permute-start.1 = (f32[2,4,2,16,128]{4,3,2,1,0:T(8,128)S(1)}, f32[2,4,2,16,128]{4,3,2,1,0:T(8,128)S(1)}, u32[]{:S(2)}, u32[]{:S(2)}) collective-permute-start(f32[2,4,2,16,128]{4,3,2,1,0:T(8,128)S(1)} %pad_maximum_fusion.surf_own), channel_id=1, source_target_pairs={{0,1},{1,0},{2,3},{3,2},{4,5},{5,4},{6,7},{7,6},{8,9},{9,8},{10,11... | collective-permute-start | bytes 393224 | tf_op jit(solution)/shard_map/ppermute | solution.py:49
  14.2 1.0 %collective-permute-done.1.surf_other = f32[2,4,2,16,128]{4,3,2,1,0:T(8,128)S(1)} collective-permute-done((f32[2,4,2,16,128]{4,3,2,1,0:T(8,128)S(1)}, f32[2,4,2,16,128]{4,3,2,1,0:T(8,128)S(1)}, u32[]{:S(2)}, u32[]{:S(2)}) %collective-permute-start.1) | collective-permute-done | bytes 131104 | tf_op jit(solution)/shard_map/ppermute | solution.py:49
  15.2 0.0 collective-permute-done.8.bins_other
  15.2 0.0 copy-done
  15.2 0.0 copy-done.2
  15.2 5.2 %shard_map.47 = (f32[96,128]{1,0:T(8,128)S(1)}, f32[96,128]{1,0:T(8,128)S(1)}, s32[2,16]{1,0:T(2,128)S(1)}) custom-call(f32[13,2,2,128]{3,2,1,0:T(2,128)S(1)} %copy-done, s32[2,16]{1,0:T(2,128)S(1)} %bitcast.5, f32[2,4,2,16,128]{4,3,2,1,0:T(8,128)S(1)} %pad_maximum_fusion.surf_own, f32[2,4,2,16,128]{4,3,2,1,0:T(8,128)S(1)} %collective-permute-done.1.surf_other, ...), custom_call_target="tpu_custom_call" | custom-call | flops 54525952 | bytes 2394368 | tf_op jit(solution)/shard_map/pallas_call | solution.py:294
  20.4 0.4 %collective-permute-start.9 = (f32[96,128]{1,0:T(8,128)S(1)}, f32[96,128]{1,0:T(8,128)S(1)}, u32[]{:S(2)}, u32[]{:S(2)}) collective-permute-start(f32[96,128]{1,0:T(8,128)S(1)} %get-tuple-element.10), channel_id=1, source_target_pairs={{0,1},{1,0},{2,3},{3,2},{4,5},{5,4},{6,7},{7,6},{8,9},{9,8},{10,11... | collective-permute-start | bytes 147464 | tf_op jit(solution)/shard_map/ppermute | solution.py:49
  20.8 0.9 %collective-permute-done.9.other = f32[96,128]{1,0:T(8,128)S(1)} collective-permute-done((f32[96,128]{1,0:T(8,128)S(1)}, f32[96,128]{1,0:T(8,128)S(1)}, u32[]{:S(2)}, u32[]{:S(2)}) %collective-permute-start.9) | collective-permute-done | bytes 49184 | tf_op jit(solution)/shard_map/ppermute | solution.py:49
  21.7 1.0 %imaging.1 = f32[1,16,16,128]{3,2,1,0:T(8,128)} custom-call(s32[2,16]{1,0:T(2,128)S(1)} %get-tuple-element.8.offsets, f32[96,128]{1,0:T(8,128)S(1)} %get-tuple-element.9.mine, f32[96,128]{1,0:T(8,128)S(1)} %collective-permute-done.9.other), custom_call_target="tpu_custom_call" | custom-call | tf_op jit(solution)/shard_map/imaging/pallas_call | solution.py:360
  (10 shorter events, 0.1 us)
Async XLA Ops:
  0.0 5.4 %collective-permute-start.2 = (s32[1,2,16,128]{3,2,1,0:T(8,128)}, s32[1,2,16,128]{3,2,1,0:T(8,128)S(1)}, u32[]{:S(2)}, u32[]{:S(2)}) collective-permute-start(s32[1,2,16,128]{3,2,1,0:T(8,128)} %bins.1), channel_id=1, source_target_pairs={{0,17},{1,16},{2,19},{3,18},{4,21},{5,20},{6,23},{7,22},{8,25},{9,... | collective-permute-start | bytes 49160 | tf_op jit(solution)/shard_map/ppermute | solution.py:49
  0.6 4.8 %collective-permute-start.4 = (s32[1,2,16,128]{3,2,1,0:T(8,128)}, s32[1,2,16,128]{3,2,1,0:T(8,128)S(1)}, u32[]{:S(2)}, u32[]{:S(2)}) collective-permute-start(s32[1,2,16,128]{3,2,1,0:T(8,128)} %bins.1), channel_id=1, source_target_pairs={{0,24},{1,25},{2,26},{3,27},{4,28},{5,29},{6,30},{7,31},{8,16},{9,... | collective-permute-start | bytes 49160 | tf_op jit(solution)/shard_map/ppermute | solution.py:49
  2.8 3.7 %collective-permute-start.3 = (s32[1,2,16,128]{3,2,1,0:T(8,128)}, s32[1,2,16,128]{3,2,1,0:T(8,128)S(1)}, u32[]{:S(2)}, u32[]{:S(2)}) collective-permute-start(s32[1,2,16,128]{3,2,1,0:T(8,128)} %bins.1), channel_id=1, source_target_pairs={{0,9},{1,8},{2,11},{3,10},{4,13},{5,12},{6,15},{7,14},{8,1},{9,0},... | collective-permute-start | bytes 49160 | tf_op jit(solution)/shard_map/ppermute | solution.py:49
  3.2 10.2 %collective-permute-start = (f32[1,4,2,16,128]{4,3,2,1,0:T(8,128)}, f32[1,4,2,16,128]{4,3,2,1,0:T(8,128)S(1)}, u32[]{:S(2)}, u32[]{:S(2)}) collective-permute-start(f32[1,4,2,16,128]{4,3,2,1,0:T(8,128)} %bitcast.7), channel_id=1, source_target_pairs={{0,3},{1,2},{2,1},{3,0},{4,7},{5,6},{6,5},{7,4},{8,11},{9,10},{10,... | collective-permute-start | bytes 196616 | tf_op jit(solution)/shard_map/ppermute | solution.py:49
  4.7 0.7 %copy-start.1 = (s32[1,2,16,128]{3,2,1,0:T(8,128)S(1)}, s32[1,2,16,128]{3,2,1,0:T(8,128)}, u32[]{:S(2)}) copy-start(s32[1,2,16,128]{3,2,1,0:T(8,128)} %bins.1) | copy-start | bytes 49156
  6.5 4.5 %collective-permute-start.7 = (s32[4,2,16,128]{3,2,1,0:T(8,128)S(1)}, s32[4,2,16,128]{3,2,1,0:T(8,128)S(1)}, u32[]{:S(2)}, u32[]{:S(2)}) collective-permute-start(s32[4,2,16,128]{3,2,1,0:T(8,128)S(1)} %pad_add_fusion.1), channel_id=1, source_target_pairs={{0,6},{1,7},{2,4},{3,5},{4,2},{5,3},{6,0},{7,1},{8,14},{9,15},{10,... | collective-permute-start | bytes 196616 | tf_op jit(solution)/shard_map/ppermute | solution.py:49
  7.6 4.3 %collective-permute-start.6 = (s32[4,2,16,128]{3,2,1,0:T(8,128)S(1)}, s32[4,2,16,128]{3,2,1,0:T(8,128)S(1)}, u32[]{:S(2)}, u32[]{:S(2)}) collective-permute-start(s32[4,2,16,128]{3,2,1,0:T(8,128)S(1)} %pad_add_fusion.1), channel_id=1, source_target_pairs={{0,3},{1,2},{2,1},{3,0},{4,7},{5,6},{6,5},{7,4},{8,11},{9,10},{10,... | collective-permute-start | bytes 196616 | tf_op jit(solution)/shard_map/ppermute | solution.py:49
  8.1 4.7 %collective-permute-start.5 = (s32[4,2,16,128]{3,2,1,0:T(8,128)S(1)}, s32[4,2,16,128]{3,2,1,0:T(8,128)S(1)}, u32[]{:S(2)}, u32[]{:S(2)}) collective-permute-start(s32[4,2,16,128]{3,2,1,0:T(8,128)S(1)} %pad_add_fusion.1), channel_id=1, source_target_pairs={{0,5},{1,4},{2,7},{3,6},{4,1},{5,0},{6,3},{7,2},{8,13},{9,12},{10,... | collective-permute-start | bytes 196616 | tf_op jit(solution)/shard_map/ppermute | solution.py:49
  12.9 0.8 %copy-start.3 = (f32[2,2,2,16,128]{4,3,2,1,0:T(8,128)S(1)}, f32[2,2,2,16,128]{4,3,2,1,0:T(8,128)}, u32[]{:S(2)}) copy-start(f32[2,2,2,16,128]{4,3,2,1,0:T(8,128)} %param.4) | copy-start | bytes 196612
  12.9 2.3 %copy-start = (f32[13,2,2,128]{3,2,1,0:T(2,128)S(1)}, f32[13,2,2,128]{3,2,1,0:T(2,128)}, u32[]{:S(2)}) copy-start(f32[13,2,2,128]{3,2,1,0:T(2,128)} %table.1) | copy-start | bytes 79876
  12.9 2.3 %collective-permute-start.8 = (s32[2,8,2,16,128]{4,3,2,1,0:T(8,128)S(1)}, s32[2,8,2,16,128]{4,3,2,1,0:T(8,128)S(1)}, u32[]{:S(2)}, u32[]{:S(2)}) collective-permute-start(s32[2,8,2,16,128]{4,3,2,1,0:T(8,128)S(1)} %pad_add_fusion.bins_own), channel_id=1, source_target_pairs={{0,1},{1,0},{2,3},{3,2},{4,5},{5,4},{6,7},{7,6},{8,9},{9,8},{10,11... | collective-permute-start | bytes 786440 | tf_op jit(solution)/shard_map/ppermute | solution.py:49
  13.7 1.5 %copy-start.2 = (s32[16,2]{0,1:T(2,128)S(1)}, s32[16,2]{0,1:T(2,128)}, u32[]{:S(2)}) copy-start(s32[16,2]{0,1:T(2,128)} %param.7) | copy-start | bytes 388
  13.7 1.4 %collective-permute-start.1 = (f32[2,4,2,16,128]{4,3,2,1,0:T(8,128)S(1)}, f32[2,4,2,16,128]{4,3,2,1,0:T(8,128)S(1)}, u32[]{:S(2)}, u32[]{:S(2)}) collective-permute-start(f32[2,4,2,16,128]{4,3,2,1,0:T(8,128)S(1)} %pad_maximum_fusion.surf_own), channel_id=1, source_target_pairs={{0,1},{1,0},{2,3},{3,2},{4,5},{5,4},{6,7},{7,6},{8,9},{9,8},{10,11... | collective-permute-start | bytes 393224 | tf_op jit(solution)/shard_map/ppermute | solution.py:49
  20.4 1.3 %collective-permute-start.9 = (f32[96,128]{1,0:T(8,128)S(1)}, f32[96,128]{1,0:T(8,128)S(1)}, u32[]{:S(2)}, u32[]{:S(2)}) collective-permute-start(f32[96,128]{1,0:T(8,128)S(1)} %get-tuple-element.10), channel_id=1, source_target_pairs={{0,1},{1,0},{2,3},{3,2},{4,5},{5,4},{6,7},{7,6},{8,9},{9,8},{10,11... | collective-permute-start | bytes 147464 | tf_op jit(solution)/shard_map/ppermute | solution.py:49

commit v2 on v1

--- a/solution.py
+++ b/solution.py
@@ -255,7 +255,8 @@
             out[below : below + tall, :] = first[2 * freqs + array, pl.ds(above, tall), :]
 
 
-def image_kernel(freqs, offsets, mine, other, image):
+def image_kernel(freqs, offsets, pack, *images):
+    image = images[-1]
     row_count, width = image.shape[2:]
     tall = row_count + 2 * OFF_Y
     lanes = lax.broadcasted_iota(jnp.int32, (row_count, width), 1)
@@ -264,16 +265,16 @@
         dx = offsets[1, h]
         valid = (lanes + dx >= 0) & (lanes + dx < width)
         total = None
-        for pack in (mine, other):
-            for array in range(2 * freqs):
-                source = pack[array * row_count : (array + 1) * row_count, :]
-                start = 2 * freqs * row_count + array * tall + OFF_Y
-                value = pack[pl.ds(start + dy, row_count), :]
-                term = source * pltpu.roll(value, lax.rem(width - dx, width), 1)
-                if array >= freqs:
-                    term = -term
-                total = term if total is None else total + term
-        image[0, h] = jnp.where(valid, total, 0.0)
+        for array in range(2 * freqs):
+            source = pack[array * row_count : (array + 1) * row_count, :]
+            start = 2 * freqs * row_count + array * tall + OFF_Y
+            value = pack[pl.ds(start + dy, row_count), :]
+            term = source * pltpu.roll(value, lax.rem(width - dx, width), 1)
+            if array >= freqs:
+                term = -term
+            total = term if total is None else total + term
+        total = jnp.where(valid, total, 0.0)
+        image[0, h] = total if len(images) == 1 else images[0][0, h] + total
 
 
 def shards(surface_fields, stencil_table, velocity_bins, offset_list):
@@ -357,14 +358,10 @@
         bins_other,
     )
     other = hop(theirs, 0, 1)
-    image = pl.pallas_call(
-        functools.partial(image_kernel, freqs),
-        out_shape=like((1, offset_list.shape[0], row_count, width), f32),
-        in_specs=[VMEM, VMEM, VMEM],
-        out_specs=VMEM,
-        compiler_params=pltpu.CompilerParams(vmem_limit_bytes=4 << 20),
-        name="imaging",
-    )(offsets, mine, other)
+    shape = like((1, offset_list.shape[0], row_count, width), f32)
+    imaging = functools.partial(image_kernel, freqs)
+    (partial,) = call(imaging, [shape], [], 1000, offsets, mine)
+    (image,) = call(imaging, [shape], [], 1000, offsets, other, partial)
     return image
 
 

time: 22.9 us -> 22.8 us (level)
  waiting for transfers between devices: 6.33 us -> 6.09 us
    pallas_call x2 -> x4, Pallas kernels: 5.21 us -> 6.34 us  [call(): pl.pallas_call(kernel, out_shape=outs, in_specs=[VMEM] * len(args), out_s...]
    pallas_call x1 -> x0, Pallas kernels: 0.96 us -> none  [shards(): pl.pallas_call(functools.partial(image_kernel, freqs), out_shape=like((1,...]
    ppermute x10, waiting for transfers between devices: 6.33 us -> 6.09 us  [hop(): return lax.ppermute(block, ('depth', 'xline'), route)]
  transfers between devices with their start and end apart: 10 -> 10, of which waited for: 6 -> 6; matrix products, arithmetic and copies ran while one was open for 0% -> 0% of each run, Pallas kernels for 0% -> 1%
where the time goes in v2:
time: 22.8 us; the launch traced here: 22.6 us
  starting transfers between devices  8.98 us (39%)
  Pallas kernels  6.34 us (28%)
  waiting for transfers between devices  6.09 us (27%)
  local copies, waits for them, and re-layouts  1.08 us (5%)
    ppermute x10, starting transfers between devices, hop(): return lax.ppermute(block, ('depth', 'xline'), route)  8.98 us
    pallas_call x4, Pallas kernels, call(): pl.pallas_call(kernel, out_shape=outs, in_specs=[VMEM] * len(args), out_s...  6.34 us
    ppermute x10, waiting for transfers between devices, hop(): return lax.ppermute(block, ('depth', 'xline'), route)  6.09 us
    unnamed x12, local copies, waits for them, and re-layouts  1.08 us
  transfers between devices with their start and end apart: 10, of which 6 were waited for; matrix products, arithmetic and copies ran while one was open for 0% of the time, Pallas kernels for 1%

profile of v2, /device:TPU:29, one launch (start us, length us, event | category | flops | bytes accessed | tf_op | source)
XLA Modules:
  0.0 22.6 jit_solution(7757821842464829361)
XLA Ops:
  0.0 0.6 %collective-permute-start.2 = (s32[1,2,16,128]{3,2,1,0:T(8,128)}, s32[1,2,16,128]{3,2,1,0:T(8,128)S(1)}, u32[]{:S(2)}, u32[]{:S(2)}) collective-permute-start(s32[1,2,16,128]{3,2,1,0:T(8,128)} %bins.1), channel_id=1, source_target_pairs={{0,17},{1,16},{2,19},{3,18},{4,21},{5,20},{6,23},{7,22},{8,25},{9,... | collective-permute-start | bytes 49160 | tf_op jit(solution)/shard_map/ppermute | solution.py:49
  0.6 2.2 %collective-permute-start.4 = (s32[1,2,16,128]{3,2,1,0:T(8,128)}, s32[1,2,16,128]{3,2,1,0:T(8,128)S(1)}, u32[]{:S(2)}, u32[]{:S(2)}) collective-permute-start(s32[1,2,16,128]{3,2,1,0:T(8,128)} %bins.1), channel_id=1, source_target_pairs={{0,24},{1,25},{2,26},{3,27},{4,28},{5,29},{6,30},{7,31},{8,16},{9,... | collective-permute-start | bytes 49160 | tf_op jit(solution)/shard_map/ppermute | solution.py:49
  2.8 0.4 %collective-permute-start.3 = (s32[1,2,16,128]{3,2,1,0:T(8,128)}, s32[1,2,16,128]{3,2,1,0:T(8,128)S(1)}, u32[]{:S(2)}, u32[]{:S(2)}) collective-permute-start(s32[1,2,16,128]{3,2,1,0:T(8,128)} %bins.1), channel_id=1, source_target_pairs={{0,9},{1,8},{2,11},{3,10},{4,13},{5,12},{6,15},{7,14},{8,1},{9,0},... | collective-permute-start | bytes 49160 | tf_op jit(solution)/shard_map/ppermute | solution.py:49
  3.2 1.5 %collective-permute-start = (f32[1,4,2,16,128]{4,3,2,1,0:T(8,128)}, f32[1,4,2,16,128]{4,3,2,1,0:T(8,128)S(1)}, u32[]{:S(2)}, u32[]{:S(2)}) collective-permute-start(f32[1,4,2,16,128]{4,3,2,1,0:T(8,128)} %bitcast.7), channel_id=1, source_target_pairs={{0,3},{1,2},{2,1},{3,0},{4,7},{5,6},{6,5},{7,4},{8,11},{9,10},{10,... | collective-permute-start | bytes 196616 | tf_op jit(solution)/shard_map/ppermute | solution.py:49
  4.7 0.0 copy-start.1
  4.7 0.7 %copy-done.1 = s32[1,2,16,128]{3,2,1,0:T(8,128)S(1)} copy-done((s32[1,2,16,128]{3,2,1,0:T(8,128)S(1)}, s32[1,2,16,128]{3,2,1,0:T(8,128)}, u32[]{:S(2)}) %copy-start.1) | copy-done | bytes 16408
  5.4 0.0 collective-permute-done.2
  5.4 0.0 collective-permute-done.4
  5.4 1.0 %collective-permute-done.3 = s32[1,2,16,128]{3,2,1,0:T(8,128)S(1)} collective-permute-done((s32[1,2,16,128]{3,2,1,0:T(8,128)}, s32[1,2,16,128]{3,2,1,0:T(8,128)S(1)}, u32[]{:S(2)}, u32[]{:S(2)}) %collective-permute-start.3) | collective-permute-done | bytes 16416 | tf_op jit(solution)/shard_map/ppermute | solution.py:49
  6.5 1.2 %collective-permute-start.7 = (s32[4,2,16,128]{3,2,1,0:T(8,128)S(1)}, s32[4,2,16,128]{3,2,1,0:T(8,128)S(1)}, u32[]{:S(2)}, u32[]{:S(2)}) collective-permute-start(s32[4,2,16,128]{3,2,1,0:T(8,128)S(1)} %pad_add_fusion.1), channel_id=1, source_target_pairs={{0,6},{1,7},{2,4},{3,5},{4,2},{5,3},{6,0},{7,1},{8,14},{9,15},{10,... | collective-permute-start | bytes 196616 | tf_op jit(solution)/shard_map/ppermute | solution.py:49
  7.6 0.5 %collective-permute-start.6 = (s32[4,2,16,128]{3,2,1,0:T(8,128)S(1)}, s32[4,2,16,128]{3,2,1,0:T(8,128)S(1)}, u32[]{:S(2)}, u32[]{:S(2)}) collective-permute-start(s32[4,2,16,128]{3,2,1,0:T(8,128)S(1)} %pad_add_fusion.1), channel_id=1, source_target_pairs={{0,3},{1,2},{2,1},{3,0},{4,7},{5,6},{6,5},{7,4},{8,11},{9,10},{10,... | collective-permute-start | bytes 196616 | tf_op jit(solution)/shard_map/ppermute | solution.py:49
  8.1 1.3 %collective-permute-start.5 = (s32[4,2,16,128]{3,2,1,0:T(8,128)S(1)}, s32[4,2,16,128]{3,2,1,0:T(8,128)S(1)}, u32[]{:S(2)}, u32[]{:S(2)}) collective-permute-start(s32[4,2,16,128]{3,2,1,0:T(8,128)S(1)} %pad_add_fusion.1), channel_id=1, source_target_pairs={{0,5},{1,4},{2,7},{3,6},{4,1},{5,0},{6,3},{7,2},{8,13},{9,12},{10,... | collective-permute-start | bytes 196616 | tf_op jit(solution)/shard_map/ppermute | solution.py:49
  9.4 1.5 %collective-permute-done.7 = s32[4,2,16,128]{3,2,1,0:T(8,128)S(1)} collective-permute-done((s32[4,2,16,128]{3,2,1,0:T(8,128)S(1)}, s32[4,2,16,128]{3,2,1,0:T(8,128)S(1)}, u32[]{:S(2)}, u32[]{:S(2)}) %collective-permute-start.7) | collective-permute-done | bytes 65568 | tf_op jit(solution)/shard_map/ppermute | solution.py:49
  11.0 1.0 %collective-permute-done.6 = s32[4,2,16,128]{3,2,1,0:T(8,128)S(1)} collective-permute-done((s32[4,2,16,128]{3,2,1,0:T(8,128)S(1)}, s32[4,2,16,128]{3,2,1,0:T(8,128)S(1)}, u32[]{:S(2)}, u32[]{:S(2)}) %collective-permute-start.6) | collective-permute-done | bytes 65568 | tf_op jit(solution)/shard_map/ppermute | solution.py:49
  12.0 0.9 %collective-permute-done.5 = s32[4,2,16,128]{3,2,1,0:T(8,128)S(1)} collective-permute-done((s32[4,2,16,128]{3,2,1,0:T(8,128)S(1)}, s32[4,2,16,128]{3,2,1,0:T(8,128)S(1)}, u32[]{:S(2)}, u32[]{:S(2)}) %collective-permute-start.5) | collective-permute-done | bytes 65568 | tf_op jit(solution)/shard_map/ppermute | solution.py:49
  12.9 0.0 copy-start.3
  12.9 0.0 copy-start
  12.9 0.5 %collective-permute-start.8 = (s32[2,8,2,16,128]{4,3,2,1,0:T(8,128)S(1)}, s32[2,8,2,16,128]{4,3,2,1,0:T(8,128)S(1)}, u32[]{:S(2)}, u32[]{:S(2)}) collective-permute-start(s32[2,8,2,16,128]{4,3,2,1,0:T(8,128)S(1)} %pad_add_fusion.bins_own), channel_id=1, source_target_pairs={{0,1},{1,0},{2,3},{3,2},{4,5},{5,4},{6,7},{7,6},{8,9},{9,8},{10,11... | collective-permute-start | bytes 786440 | tf_op jit(solution)/shard_map/ppermute | solution.py:49
  13.4 0.0 collective-permute-done
  13.4 0.3 %copy-done.3 = f32[2,2,2,16,128]{4,3,2,1,0:T(8,128)S(1)} copy-done((f32[2,2,2,16,128]{4,3,2,1,0:T(8,128)S(1)}, f32[2,2,2,16,128]{4,3,2,1,0:T(8,128)}, u32[]{:S(2)}) %copy-start.3) | copy-done | bytes 65560
  13.7 0.0 copy-start.2
  13.7 0.5 %collective-permute-start.1 = (f32[2,4,2,16,128]{4,3,2,1,0:T(8,128)S(1)}, f32[2,4,2,16,128]{4,3,2,1,0:T(8,128)S(1)}, u32[]{:S(2)}, u32[]{:S(2)}) collective-permute-start(f32[2,4,2,16,128]{4,3,2,1,0:T(8,128)S(1)} %pad_maximum_fusion.surf_own), channel_id=1, source_target_pairs={{0,1},{1,0},{2,3},{3,2},{4,5},{5,4},{6,7},{7,6},{8,9},{9,8},{10,11... | collective-permute-start | bytes 393224 | tf_op jit(solution)/shard_map/ppermute | solution.py:49
  14.2 1.0 %collective-permute-done.1.surf_other = f32[2,4,2,16,128]{4,3,2,1,0:T(8,128)S(1)} collective-permute-done((f32[2,4,2,16,128]{4,3,2,1,0:T(8,128)S(1)}, f32[2,4,2,16,128]{4,3,2,1,0:T(8,128)S(1)}, u32[]{:S(2)}, u32[]{:S(2)}) %collective-permute-start.1) | collective-permute-done | bytes 131104 | tf_op jit(solution)/shard_map/ppermute | solution.py:49
  15.2 0.0 collective-permute-done.8.bins_other
  15.2 0.0 copy-done
  15.2 0.0 copy-done.2
  15.2 5.2 %shard_map.47 = (f32[96,128]{1,0:T(8,128)S(1)}, f32[96,128]{1,0:T(8,128)S(1)}, s32[2,16]{1,0:T(2,128)S(1)}) custom-call(f32[13,2,2,128]{3,2,1,0:T(2,128)S(1)} %copy-done, s32[2,16]{1,0:T(2,128)S(1)} %bitcast.5, f32[2,4,2,16,128]{4,3,2,1,0:T(8,128)S(1)} %pad_maximum_fusion.surf_own, f32[2,4,2,16,128]{4,3,2,1,0:T(8,128)S(1)} %collective-permute-done.1.surf_other, ...), custom_call_target="tpu_custom_call" | custom-call | flops 54525952 | bytes 2394368 | tf_op jit(solution)/shard_map/pallas_call | solution.py:295
  20.4 0.4 %collective-permute-start.9 = (f32[96,128]{1,0:T(8,128)S(1)}, f32[96,128]{1,0:T(8,128)S(1)}, u32[]{:S(2)}, u32[]{:S(2)}) collective-permute-start(f32[96,128]{1,0:T(8,128)S(1)} %get-tuple-element.9), channel_id=1, source_target_pairs={{0,1},{1,0},{2,3},{3,2},{4,5},{5,4},{6,7},{7,6},{8,9},{9,8},{10,11... | collective-permute-start | bytes 147464 | tf_op jit(solution)/shard_map/ppermute | solution.py:49
  20.8 0.2 %shard_map.48.images_0_ = f32[1,16,16,128]{3,2,1,0:T(8,128)S(1)} custom-call(s32[2,16]{1,0:T(2,128)S(1)} %get-tuple-element.8.offsets, f32[96,128]{1,0:T(8,128)S(1)} %get-tuple-element.10.pack), custom_call_target="tpu_custom_call" | custom-call | flops 1000 | bytes 180352 | tf_op jit(solution)/shard_map/pallas_call | solution.py:295
  21.1 0.6 %collective-permute-done.9.pack = f32[96,128]{1,0:T(8,128)S(1)} collective-permute-done((f32[96,128]{1,0:T(8,128)S(1)}, f32[96,128]{1,0:T(8,128)S(1)}, u32[]{:S(2)}, u32[]{:S(2)}) %collective-permute-start.9) | collective-permute-done | bytes 49184 | tf_op jit(solution)/shard_map/ppermute | solution.py:49
  21.7 0.9 %shard_map.49 = f32[1,16,16,128]{3,2,1,0:T(8,128)} custom-call(s32[2,16]{1,0:T(2,128)S(1)} %get-tuple-element.8.offsets, f32[96,128]{1,0:T(8,128)S(1)} %collective-permute-done.9.pack, f32[1,16,16,128]{3,2,1,0:T(8,128)S(1)} %shard_map.48.images_0_), custom_call_target="tpu_custom_call" | custom-call | flops 1000 | bytes 311424 | tf_op jit(solution)/shard_map/pallas_call | solution.py:295
  (10 shorter events, 0.1 us)
Async XLA Ops:
  0.0 5.4 %collective-permute-start.2 = (s32[1,2,16,128]{3,2,1,0:T(8,128)}, s32[1,2,16,128]{3,2,1,0:T(8,128)S(1)}, u32[]{:S(2)}, u32[]{:S(2)}) collective-permute-start(s32[1,2,16,128]{3,2,1,0:T(8,128)} %bins.1), channel_id=1, source_target_pairs={{0,17},{1,16},{2,19},{3,18},{4,21},{5,20},{6,23},{7,22},{8,25},{9,... | collective-permute-start | bytes 49160 | tf_op jit(solution)/shard_map/ppermute | solution.py:49
  0.6 4.8 %collective-permute-start.4 = (s32[1,2,16,128]{3,2,1,0:T(8,128)}, s32[1,2,16,128]{3,2,1,0:T(8,128)S(1)}, u32[]{:S(2)}, u32[]{:S(2)}) collective-permute-start(s32[1,2,16,128]{3,2,1,0:T(8,128)} %bins.1), channel_id=1, source_target_pairs={{0,24},{1,25},{2,26},{3,27},{4,28},{5,29},{6,30},{7,31},{8,16},{9,... | collective-permute-start | bytes 49160 | tf_op jit(solution)/shard_map/ppermute | solution.py:49
  2.8 3.7 %collective-permute-start.3 = (s32[1,2,16,128]{3,2,1,0:T(8,128)}, s32[1,2,16,128]{3,2,1,0:T(8,128)S(1)}, u32[]{:S(2)}, u32[]{:S(2)}) collective-permute-start(s32[1,2,16,128]{3,2,1,0:T(8,128)} %bins.1), channel_id=1, source_target_pairs={{0,9},{1,8},{2,11},{3,10},{4,13},{5,12},{6,15},{7,14},{8,1},{9,0},... | collective-permute-start | bytes 49160 | tf_op jit(solution)/shard_map/ppermute | solution.py:49
  3.2 10.2 %collective-permute-start = (f32[1,4,2,16,128]{4,3,2,1,0:T(8,128)}, f32[1,4,2,16,128]{4,3,2,1,0:T(8,128)S(1)}, u32[]{:S(2)}, u32[]{:S(2)}) collective-permute-start(f32[1,4,2,16,128]{4,3,2,1,0:T(8,128)} %bitcast.7), channel_id=1, source_target_pairs={{0,3},{1,2},{2,1},{3,0},{4,7},{5,6},{6,5},{7,4},{8,11},{9,10},{10,... | collective-permute-start | bytes 196616 | tf_op jit(solution)/shard_map/ppermute | solution.py:49
  4.7 0.7 %copy-start.1 = (s32[1,2,16,128]{3,2,1,0:T(8,128)S(1)}, s32[1,2,16,128]{3,2,1,0:T(8,128)}, u32[]{:S(2)}) copy-start(s32[1,2,16,128]{3,2,1,0:T(8,128)} %bins.1) | copy-start | bytes 49156
  6.5 4.5 %collective-permute-start.7 = (s32[4,2,16,128]{3,2,1,0:T(8,128)S(1)}, s32[4,2,16,128]{3,2,1,0:T(8,128)S(1)}, u32[]{:S(2)}, u32[]{:S(2)}) collective-permute-start(s32[4,2,16,128]{3,2,1,0:T(8,128)S(1)} %pad_add_fusion.1), channel_id=1, source_target_pairs={{0,6},{1,7},{2,4},{3,5},{4,2},{5,3},{6,0},{7,1},{8,14},{9,15},{10,... | collective-permute-start | bytes 196616 | tf_op jit(solution)/shard_map/ppermute | solution.py:49
  7.6 4.3 %collective-permute-start.6 = (s32[4,2,16,128]{3,2,1,0:T(8,128)S(1)}, s32[4,2,16,128]{3,2,1,0:T(8,128)S(1)}, u32[]{:S(2)}, u32[]{:S(2)}) collective-permute-start(s32[4,2,16,128]{3,2,1,0:T(8,128)S(1)} %pad_add_fusion.1), channel_id=1, source_target_pairs={{0,3},{1,2},{2,1},{3,0},{4,7},{5,6},{6,5},{7,4},{8,11},{9,10},{10,... | collective-permute-start | bytes 196616 | tf_op jit(solution)/shard_map/ppermute | solution.py:49
  8.1 4.7 %collective-permute-start.5 = (s32[4,2,16,128]{3,2,1,0:T(8,128)S(1)}, s32[4,2,16,128]{3,2,1,0:T(8,128)S(1)}, u32[]{:S(2)}, u32[]{:S(2)}) collective-permute-start(s32[4,2,16,128]{3,2,1,0:T(8,128)S(1)} %pad_add_fusion.1), channel_id=1, source_target_pairs={{0,5},{1,4},{2,7},{3,6},{4,1},{5,0},{6,3},{7,2},{8,13},{9,12},{10,... | collective-permute-start | bytes 196616 | tf_op jit(solution)/shard_map/ppermute | solution.py:49
  12.9 0.8 %copy-start.3 = (f32[2,2,2,16,128]{4,3,2,1,0:T(8,128)S(1)}, f32[2,2,2,16,128]{4,3,2,1,0:T(8,128)}, u32[]{:S(2)}) copy-start(f32[2,2,2,16,128]{4,3,2,1,0:T(8,128)} %param.4) | copy-start | bytes 196612
  12.9 2.3 %copy-start = (f32[13,2,2,128]{3,2,1,0:T(2,128)S(1)}, f32[13,2,2,128]{3,2,1,0:T(2,128)}, u32[]{:S(2)}) copy-start(f32[13,2,2,128]{3,2,1,0:T(2,128)} %table.1) | copy-start | bytes 79876
  12.9 2.3 %collective-permute-start.8 = (s32[2,8,2,16,128]{4,3,2,1,0:T(8,128)S(1)}, s32[2,8,2,16,128]{4,3,2,1,0:T(8,128)S(1)}, u32[]{:S(2)}, u32[]{:S(2)}) collective-permute-start(s32[2,8,2,16,128]{4,3,2,1,0:T(8,128)S(1)} %pad_add_fusion.bins_own), channel_id=1, source_target_pairs={{0,1},{1,0},{2,3},{3,2},{4,5},{5,4},{6,7},{7,6},{8,9},{9,8},{10,11... | collective-permute-start | bytes 786440 | tf_op jit(solution)/shard_map/ppermute | solution.py:49
  13.7 1.5 %copy-start.2 = (s32[16,2]{0,1:T(2,128)S(1)}, s32[16,2]{0,1:T(2,128)}, u32[]{:S(2)}) copy-start(s32[16,2]{0,1:T(2,128)} %param.7) | copy-start | bytes 388
  13.7 1.4 %collective-permute-start.1 = (f32[2,4,2,16,128]{4,3,2,1,0:T(8,128)S(1)}, f32[2,4,2,16,128]{4,3,2,1,0:T(8,128)S(1)}, u32[]{:S(2)}, u32[]{:S(2)}) collective-permute-start(f32[2,4,2,16,128]{4,3,2,1,0:T(8,128)S(1)} %pad_maximum_fusion.surf_own), channel_id=1, source_target_pairs={{0,1},{1,0},{2,3},{3,2},{4,5},{5,4},{6,7},{7,6},{8,9},{9,8},{10,11... | collective-permute-start | bytes 393224 | tf_op jit(solution)/shard_map/ppermute | solution.py:49
  20.4 1.3 %collective-permute-start.9 = (f32[96,128]{1,0:T(8,128)S(1)}, f32[96,128]{1,0:T(8,128)S(1)}, u32[]{:S(2)}, u32[]{:S(2)}) collective-permute-start(f32[96,128]{1,0:T(8,128)S(1)} %get-tuple-element.9), channel_id=1, source_target_pairs={{0,1},{1,0},{2,3},{3,2},{4,5},{5,4},{6,7},{7,6},{8,9},{9,8},{10,11... | collective-permute-start | bytes 147464 | tf_op jit(solution)/shard_map/ppermute | solution.py:49
